TPU v7x, 256 devices: a whole 4x4x8 slice. The times are simulated.
256 devices in a mesh: tm: 8 (over z), lat: 32 (over y, x, core).
Axes of the slice: x: 4, y: 4, z: 8, core: 2. Of those that a mesh axis runs over, the one named last changes fastest.
Arguments:
- wind_east: bfloat16 [960, 256, 1440], P('tm', 'lat'), may hold values from -40 to 40
- wind_north: bfloat16 [960, 256, 1440], P('tm', 'lat'), may hold values from -40 to 40
- snap_counts: int32 [8], P('tm'), may hold values from 1 to 120, 320 in all
- snap_ids: int32 [960], P('tm'), may hold values from 0 to 8759
Outputs:
- basis: bfloat16 [32, 256, 1440], P(None, 'lat')
- coeffs: float32 [32, 960], P(None, 'tm')
Inputs may be any that keep to these rules, and one draw needn't show every extreme that they name: `snap_counts`: entry b counts the used slots of the b-th block of 120 slots, which are that block's first ones; the entries sum to 320 and one of them equals 120.
All inputs are finite; a program needn't handle non-finite values.
Results may differ from a plain program's by a relative error of at most 0.0072.
Values may be sent and summed in bfloat16 or wider, within the bound.
A program may use at most 64 MiB of HBM per device.

v0:
```python
import jax
import jax.numpy as jnp
from jax import lax
from jax.sharding import PartitionSpec as P

RANK = 32


def with_halo(cells, sides, width):
    for axis, dim in sides:
        count = lax.axis_size(axis)
        ends = count - 1
        head = lax.slice_in_dim(cells, 0, width, axis=dim)
        tail = lax.slice_in_dim(cells, cells.shape[dim] - width, cells.shape[dim], axis=dim)
        cells = jnp.concatenate(
            [
                lax.ppermute(tail, axis, [(i, (i + 1) % count) for i in range(ends)]),
                cells,
                lax.ppermute(head, axis, [((i + 1) % count, i) for i in range(ends)]),
            ],
            axis=dim,
        )
    return cells


def latitude_cosine(first_row, row_count, total_rows):
    row_index = first_row + jnp.arange(row_count, dtype=jnp.int32)
    return jnp.cos((total_rows // 2 - row_index).astype(jnp.float32) * (jnp.pi / 720.0))


def sign_table(snap_ids, rank_count):
    column = jnp.arange(rank_count, dtype=jnp.int32)
    mixed = snap_ids[:, None] * 1103515245 + column[None, :] * 40503 + 12345
    mixed = jnp.bitwise_xor(mixed, jnp.right_shift(mixed, 13))
    mixed = mixed * 1664525 + 1013904223
    mixed = jnp.bitwise_xor(mixed, jnp.right_shift(mixed, 16))
    flipped = jnp.bitwise_and(jnp.right_shift(mixed, 7), 1)
    return (1 - 2 * flipped).astype(jnp.bfloat16)


def metric_vorticity(padded_east, wind_north, padded_cosine, valid):
    scaled = padded_east.astype(jnp.float32) * padded_cosine[None, :, None]
    north_side = scaled[:, :-2]
    south_side = scaled[:, 2:]
    meridional = wind_north.astype(jnp.float32)
    zonal_diff = jnp.roll(meridional, -1, axis=2) - jnp.roll(meridional, 1, axis=2)
    weight = 0.5 / jnp.sqrt(padded_cosine[1:-1])
    field = (zonal_diff - north_side + south_side) * weight[None, :, None] * valid[:, None, None]
    return field.astype(jnp.bfloat16)


def local_gram(sketch, cell_total):
    return (
        lax.dot_general(
            sketch,
            sketch,
            (((1,), (1,)), ((), ())),
            precision=lax.Precision.HIGHEST,
            preferred_element_type=jnp.float32,
        )
        / cell_total
    )


def orthonormal(gram_sum, sketch):
    factor = jnp.linalg.cholesky(gram_sum)
    inverse = lax.linalg.triangular_solve(
        factor, jnp.eye(gram_sum.shape[0], dtype=jnp.float32), left_side=True, lower=True
    )
    return jnp.dot(
        inverse, sketch, precision=lax.Precision.HIGHEST, preferred_element_type=jnp.float32
    ).astype(jnp.bfloat16)


def local(wind_east, wind_north, snap_counts, snap_ids):
    snap_slots, band_rows, lon_count = wind_east.shape
    band_count = lax.axis_size("lat")
    first_row = lax.axis_index("lat") * band_rows - 1
    padded_cosine = latitude_cosine(first_row, band_rows + 2, band_rows * band_count)
    valid = (jnp.arange(snap_slots, dtype=jnp.int32) < snap_counts[0]).astype(jnp.float32)
    padded_east = with_halo(wind_east, (("lat", 1),), 1)
    field = metric_vorticity(padded_east, wind_north, padded_cosine, valid).reshape(
        snap_slots, band_rows * lon_count
    )
    signs_matrix = sign_table(snap_ids, RANK)
    sketch = jnp.dot(signs_matrix.T, field, preferred_element_type=jnp.float32)
    cell_total = band_rows * band_count * lon_count
    sketch = lax.psum(sketch, "tm")
    gram_sum = lax.psum(local_gram(sketch, cell_total), "lat")
    basis_flat = orthonormal(gram_sum, sketch)
    projected = (
        lax.dot_general(
            basis_flat, field, (((1,), (1,)), ((), ())), preferred_element_type=jnp.float32
        )
        / cell_total
    )
    coeffs = lax.psum(projected, "lat")
    return (basis_flat.reshape(basis_flat.shape[0], band_rows, lon_count), coeffs)


def solution(mesh):
    in_specs = (P("tm", "lat", None), P("tm", "lat", None), P("tm"), P("tm"))
    out_specs = (P(None, "lat", None), P(None, "tm"))
    return jax.shard_map(local, mesh=mesh, in_specs=in_specs, out_specs=out_specs, check_vma=False)
```

profile of v0, /device:TPU:32, one launch (start us, length us, event | category | flops | bytes accessed | tf_op | source)
XLA Modules:
  0.0 398.7 jit_solution(5653867448975015679)
XLA Ops:
  7.2 0.0 copy-start
  7.2 0.0 all-reduce.2.cloned.1.call-start
  7.2 4.0 %fusion.36 = (bf16[120,1,1440]{2,1,0:T(2,128)(2,1)S(1)}, bf16[120,1,1440]{2,1,0:T(2,128)(2,1)S(1)}) fusion(bf16[120,8,1440]{2,1,0:T(8,128)(2,1)} %param.4), kind=kLoop, calls=%fused_computation.55 | loop fusion | bytes 1382400 | tf_op jit(solution)/shard_map/slice | solution.py:14
  11.2 0.8 copy.21
  12.0 2.5 collective-permute-start
  14.5 0.8 copy.22
  15.3 1.3 collective-permute-start.1
  16.7 0.0 copy-done
  16.7 0.0 copy-start.3
  16.7 6.0 %fusion.35 = (f32[120,8,1439]{2,1,0:T(8,128)}, f32[120,8,1439]{2,1,0:T(8,128)}) fusion(bf16[120,8,1440]{2,1,0:T(8,128)(2,1)S(1)} %copy-done), kind=kLoop, calls=%fused_computation.54 | loop fusion | bytes 22103040 | tf_op jit(solution)/shard_map/jit(_roll_static)/slice | solution.py:46
  22.7 0.0 copy-start.1
  22.7 0.1 rsqrt_multiply_fusion
  23.6 0.0 copy-done.3
  23.6 0.9 fusion.34
  24.5 0.0 collective-permute-done
  24.5 1.6 copy.16
  26.0 0.0 collective-permute-done.1
  26.1 0.0 slice-start
  26.1 1.7 copy.17
  27.8 0.0 copy-done.1
  27.8 0.0 slice-start.1
  27.8 0.0 copy-start.2
  27.8 3.5 convert_multiply_fusion
  31.3 0.0 slice-done
  31.3 0.0 slice-done.1
  31.3 0.0 copy-done.2
  31.4 6.7 %fusion.2 = bf16[120,8,1440]{2,1,0:T(8,128)(2,1)} fusion(f32[120,10,1440]{2,1,0:T(8,128)S(1)} %convert_multiply_fusion, f32[120,8,1]{2,1,0:T(8,128)S(1)} %copy-done.2, f32[120,8,1439]{2,1,0:T(8,128)} %get-tuple-element.5, f32[120,8,1439]{2,1,0:T(8,128)S(1)} %bitcast.19, f32[120,8,1]{2,1,0:T(8,128)S(1)} %get-tuple-element.2, f32[120]{0:T(128)S(1)} %compare_convert_fusion, ...), kind=kLoop, calls=%fused_computation.5 | loop fusion | flops 11059200 | bytes 24883712 | tf_op jit(solution)/shard_map/convert_element_type | solution.py:49
  38.0 5.6 %reshape.40 = bf16[120,11520]{1,0:T(8,128)(2,1)S(1)} reshape(bf16[120,8,1440]{2,1,0:T(8,128)(2,1)} %fusion.2) | data formatting | bytes 5529600 | tf_op jit(solution)/shard_map/reshape | solution.py:82
  43.7 1.7 fusion.14
  45.4 0.0 all-reduce.2.cloned.1.call-update
  45.4 82.4 %all-reduce.2.cloned.1.call-done = f32[32,11520]{1,0:T(8,128)} async-done(((f32[32,11520]{1,0:T(8,128)}), f32[32,11520]{1,0:T(8,128)}) %all-reduce.2.cloned.1.call-update) | async-done | bytes 1474576 | tf_op jit(solution)/shard_map/psum | solution.py:88
  127.8 3.2 convolution_multiply_fusion.1
  131.0 124.3 %psum.22 = f32[32,32]{0,1:T(8,128)S(1)} all-reduce(f32[32,32]{0,1:T(8,128)S(1)} %convolution_multiply_fusion.1), channel_id=1, replica_groups=mesh['tm'=8,'lat'=32] {'lat'}, use_global_device_ids=true, to_apply=%region_1.2 | all-reduce | flops 1024 | bytes 8192 | tf_op jit(solution)/shard_map/psum | solution.py:89
  255.3 0.1 copy.19
  255.4 2.9 cholesky.17
  258.3 0.6 compare_reduce_fusion
  259.0 0.7 fusion.3
  259.6 2.4 custom-call.6
  262.1 0.2 fusion.11
  262.3 2.7 convolution_convert_fusion
  265.0 0.9 convolution_multiply_fusion
  266.0 2.1 reshape.41
  268.1 123.8 %psum.23 = f32[32,120]{1,0:T(8,128)} all-reduce(f32[32,120]{1,0:T(8,128)S(1)} %convolution_multiply_fusion), channel_id=1, replica_groups=mesh['tm'=8,'lat'=32] {'lat'}, use_global_device_ids=true, to_apply=%region_4.5 | all-reduce | flops 3840 | bytes 30720 | tf_op jit(solution)/shard_map/psum | solution.py:97
  (7 shorter events, 0.1 us)
Async XLA Ops:
  7.2 9.5 %copy-start = (bf16[120,8,1440]{2,1,0:T(8,128)(2,1)S(1)}, bf16[120,8,1440]{2,1,0:T(8,128)(2,1)}, u32[]{:S(2)}) copy-start(bf16[120,8,1440]{2,1,0:T(8,128)(2,1)} %param.5) | copy-start | bytes 8294404
  7.2 120.6 %all-reduce.2.cloned.1.call-start = ((), (), s32[]{:S(2)}) async-start(), calls=%async_computation | async-start | bytes 2949120 | tf_op jit(solution)/shard_map/psum | solution.py:88
  12.0 12.4 %collective-permute-start = (bf16[120,1,1440]{2,0,1:T(8,128)(2,1)}, bf16[120,1,1440]{2,0,1:T(8,128)(2,1)}, u32[]{:S(2)}, u32[]{:S(2)}) collective-permute-start(bf16[120,1,1440]{2,0,1:T(8,128)(2,1)} %copy.21), channel_id=1, source_target_pairs={{0,1},{1,2},{2,3},{3,4},{4,5},{5,6},{6,7},{7,8},{8,9},{9,10},{10,1... | collective-permute-start | bytes 1036808 | tf_op jit(solution)/shard_map/ppermute | solution.py:17
  15.3 10.7 %collective-permute-start.1 = (bf16[120,1,1440]{2,0,1:T(8,128)(2,1)}, bf16[120,1,1440]{2,0,1:T(8,128)(2,1)}, u32[]{:S(2)}, u32[]{:S(2)}) collective-permute-start(bf16[120,1,1440]{2,0,1:T(8,128)(2,1)} %copy.22), channel_id=1, source_target_pairs={{1,0},{2,1},{3,2},{4,3},{5,4},{6,5},{7,6},{8,7},{9,8},{10,9},{11,1... | collective-permute-start | bytes 1036808 | tf_op jit(solution)/shard_map/ppermute | solution.py:19
  16.7 6.9 %copy-start.3 = (s32[120]{0:T(128)S(1)}, s32[120]{0:T(128)}, u32[]{:S(2)}) copy-start(s32[120]{0:T(128)} %param.7) | copy-start | bytes 1444
  22.7 5.1 %copy-start.1 = (bf16[120,8,1440]{2,1,0:T(8,128)(2,1)S(1)}, bf16[120,8,1440]{2,1,0:T(8,128)(2,1)}, u32[]{:S(2)}) copy-start(bf16[120,8,1440]{2,1,0:T(8,128)(2,1)} %param.4) | copy-start | bytes 8294404
  26.1 5.3 %slice-start = ((s8[5898240]{0:T(1024)(128)(4,1)}), s8[4194304]{0:T(1024)(128)(4,1)S(1)}, s32[]{:S(2)}) async-start(s8[5898240]{0:T(1024)(128)(4,1)} %bitcast.18), calls=%async_computation.1 | async-start | bytes 8388608
  27.8 3.5 slice-start.1
  27.8 3.5 copy-start.2
Sparse Core Ops, SparseCore 0:
  45.5 82.2 all-reduce.1
where the time goes:
time: 399 us
  blocking collectives  248 us (62%)
  waiting for transfers between devices  82.5 us (21%)
  local copies, waits for them, and re-layouts  23.6 us (6%)
  other arithmetic  17 us (4%)
  between operations  15 us (4%)
  matrix products  8.73 us (2%)
    psum x1, blocking collectives, local(): gram_sum = lax.psum(local_gram(sketch, cell_total), 'lat')  124 us
    psum x1, blocking collectives, local(): coeffs = lax.psum(projected, 'lat')  124 us
    psum x1, waiting for transfers between devices, local(): sketch = lax.psum(sketch, 'tm')  82.4 us
  transfers between devices with their start and end apart: 3, of which 1 were waited for; matrix products, arithmetic and copies ran while one was open for 2% of the time, Pallas kernels for 0%

commit v1 on v0

--- a/solution.py
+++ b/solution.py
@@ -94,7 +94,9 @@
         )
         / cell_total
     )
-    coeffs = lax.psum(projected, "lat")
+    coeffs = projected
+    for hop in (1, 2, 4, 8, 16):
+        coeffs = coeffs + lax.ppermute(coeffs, "lat", [(dev, dev ^ hop) for dev in range(32)])
     return (basis_flat.reshape(basis_flat.shape[0], band_rows, lon_count), coeffs)
 
 

time: 399 us -> 293 us (0.73)
  blocking collectives: 248 us -> 124 us
  waiting for transfers between devices: 82.5 us -> 99.5 us
    psum x1 -> x0, blocking collectives: 124 us -> none  [local(): coeffs = lax.psum(projected, 'lat')]
    ppermute x0 -> x5, waiting for transfers between devices: none -> 17.1 us  [local(): lax.ppermute(coeffs, 'lat', [(dev, dev ^ hop) for dev in range(32)])]
  transfers between devices with their start and end apart: 3 -> 8, of which waited for: 1 -> 6; matrix products, arithmetic and copies ran while one was open for 2% -> 4% of each run, Pallas kernels for 0% -> 0%
where the time goes in v1:
time: 293 us
  blocking collectives  124 us (42%)
  waiting for transfers between devices  99.5 us (34%)
  local copies, waits for them, and re-layouts  23.5 us (8%)
  other arithmetic  17.6 us (6%)
  between operations  15.1 us (5%)
  matrix products  8.72 us (3%)
  starting transfers between devices  3.91 us (1%)
    psum x1, blocking collectives, local(): gram_sum = lax.psum(local_gram(sketch, cell_total), 'lat')  124 us
    psum x1, waiting for transfers between devices, local(): sketch = lax.psum(sketch, 'tm')  82.4 us
    ppermute x5, waiting for transfers between devices, local(): lax.ppermute(coeffs, 'lat', [(dev, dev ^ hop) for dev in range(32)])  17.1 us
    slice x2, local copies, waits for them, and re-layouts, metric_vorticity(): jnp.roll(meridional, 1, axis=2)  6.83 us
    convert_element_type x1, other arithmetic, metric_vorticity(): return field.astype(jnp.bfloat16)  6.66 us
  transfers between devices with their start and end apart: 8, of which 6 were waited for; matrix products, arithmetic and copies ran while one was open for 4% of the time, Pallas kernels for 0%

profile of v1, /device:TPU:32, one launch (start us, length us, event | category | flops | bytes accessed | tf_op | source)
XLA Modules:
  0.0 292.6 jit_solution(8705762800760325848)
XLA Ops:
  7.2 0.0 copy-start
  7.2 0.0 all-reduce.2.cloned.1.call-start
  7.2 4.0 %fusion.36 = (bf16[120,1,1440]{2,1,0:T(2,128)(2,1)S(1)}, bf16[120,1,1440]{2,1,0:T(2,128)(2,1)S(1)}) fusion(bf16[120,8,1440]{2,1,0:T(8,128)(2,1)} %param.4), kind=kLoop, calls=%fused_computation.55 | loop fusion | bytes 1382400 | tf_op jit(solution)/shard_map/slice | solution.py:14
  11.2 0.8 copy.21
  12.0 2.5 collective-permute-start
  14.6 0.8 copy.22
  15.4 1.3 collective-permute-start.1
  16.7 0.0 copy-done
  16.7 0.0 copy-start.3
  16.7 6.0 %fusion.35 = (f32[120,8,1439]{2,1,0:T(8,128)}, f32[120,8,1439]{2,1,0:T(8,128)}) fusion(bf16[120,8,1440]{2,1,0:T(8,128)(2,1)S(1)} %copy-done), kind=kLoop, calls=%fused_computation.54 | loop fusion | bytes 22103040 | tf_op jit(solution)/shard_map/jit(_roll_static)/slice | solution.py:46
  22.7 0.1 rsqrt_multiply_fusion
  23.6 0.0 copy-done.3
  23.6 0.9 fusion.34
  24.5 0.0 collective-permute-done
  24.5 1.6 copy.16
  26.1 0.0 collective-permute-done.1
  26.1 0.0 slice-start
  26.1 1.7 copy.17
  27.8 0.0 slice-start.1
  27.8 0.0 copy-start.2
  27.8 3.5 %convert_multiply_fusion = f32[120,10,1440]{2,1,0:T(8,128)S(1)} fusion(bf16[120,1,1440]{2,1,0:T(2,128)(2,1)S(1)} %copy.17, bf16[120,8,1440]{2,1,0:T(8,128)(2,1)S(1)} %copy-done.1, bf16[120,1,1440]{2,1,0:T(2,128)(2,1)S(1)} %copy.16, f32[10]{0:T(128)S(1)} %multiply_cosine_fusion), kind=kLoop, calls=%fused_computation.1 | loop fusion | flops 12096000 | bytes 10368040 | tf_op jit(solution)/shard_map/mul | solution.py:42
  31.4 6.7 %fusion.2 = bf16[120,8,1440]{2,1,0:T(8,128)(2,1)} fusion(f32[120,10,1440]{2,1,0:T(8,128)S(1)} %convert_multiply_fusion, f32[120,8,1]{2,1,0:T(8,128)S(1)} %copy-done.2, f32[120,8,1439]{2,1,0:T(8,128)} %get-tuple-element.5, f32[120,8,1439]{2,1,0:T(8,128)S(1)} %bitcast.19, f32[120,8,1]{2,1,0:T(8,128)S(1)} %get-tuple-element.2, f32[120]{0:T(128)S(1)} %compare_convert_fusion, ...), kind=kLoop, calls=%fused_computation.5 | loop fusion | flops 11059200 | bytes 24883712 | tf_op jit(solution)/shard_map/convert_element_type | solution.py:49
  38.0 5.6 %reshape.40 = bf16[120,11520]{1,0:T(8,128)(2,1)S(1)} reshape(bf16[120,8,1440]{2,1,0:T(8,128)(2,1)} %fusion.2) | data formatting | bytes 5529600 | tf_op jit(solution)/shard_map/reshape | solution.py:82
  43.7 1.7 fusion.14
  45.4 0.0 all-reduce.2.cloned.1.call-update
  45.4 82.4 %all-reduce.2.cloned.1.call-done = f32[32,11520]{1,0:T(8,128)} async-done(((f32[32,11520]{1,0:T(8,128)}), f32[32,11520]{1,0:T(8,128)}) %all-reduce.2.cloned.1.call-update) | async-done | bytes 1474576 | tf_op jit(solution)/shard_map/psum | solution.py:88
  127.8 3.1 %convolution_multiply_fusion.1 = f32[32,32]{0,1:T(8,128)S(1)} fusion(f32[32,11520]{1,0:T(8,128)} %all-reduce.2.cloned.1.call-done), kind=kOutput, calls=%fused_computation.9 | convolution fusion | flops 141558784 | bytes 1478656 | tf_op jit(solution)/shard_map/dot_general | solution.py:54
  131.0 124.3 %psum.15 = f32[32,32]{0,1:T(8,128)S(1)} all-reduce(f32[32,32]{0,1:T(8,128)S(1)} %convolution_multiply_fusion.1), channel_id=1, replica_groups=mesh['tm'=8,'lat'=32] {'lat'}, use_global_device_ids=true, to_apply=%region_1.2 | all-reduce | flops 1024 | bytes 8192 | tf_op jit(solution)/shard_map/psum | solution.py:89
  255.3 0.1 copy.19
  255.4 2.9 cholesky.17
  258.3 0.6 compare_reduce_fusion
  259.0 0.7 fusion.3
  259.6 2.4 custom-call.6
  262.1 0.2 fusion.11
  262.3 2.7 convolution_convert_fusion
  265.0 0.9 convolution_multiply_fusion
  265.9 0.1 collective-permute-start.2
  266.0 1.2 collective-permute-done.2
  267.2 0.0 collective-permute-start.3
  267.2 3.7 %collective-permute-done.3 = f32[32,120]{1,0:T(8,128)S(1)} collective-permute-done((f32[32,120]{1,0:T(8,128)S(1)}, f32[32,120]{1,0:T(8,128)S(1)}, u32[]{:S(2)}, u32[]{:S(2)}) %collective-permute-start.3) | collective-permute-done | bytes 15392 | tf_op jit(solution)/shard_map/ppermute | solution.py:99
  270.9 0.0 collective-permute-start.4
  271.0 5.2 %collective-permute-done.4 = f32[32,120]{1,0:T(8,128)S(1)} collective-permute-done((f32[32,120]{1,0:T(8,128)S(1)}, f32[32,120]{1,0:T(8,128)S(1)}, u32[]{:S(2)}, u32[]{:S(2)}) %collective-permute-start.4) | collective-permute-done | bytes 15392 | tf_op jit(solution)/shard_map/ppermute | solution.py:99
  276.2 0.0 collective-permute-start.5
  276.2 3.7 %collective-permute-done.5 = f32[32,120]{1,0:T(8,128)S(1)} collective-permute-done((f32[32,120]{1,0:T(8,128)S(1)}, f32[32,120]{1,0:T(8,128)S(1)}, u32[]{:S(2)}, u32[]{:S(2)}) %collective-permute-start.5) | collective-permute-done | bytes 15392 | tf_op jit(solution)/shard_map/ppermute | solution.py:99
  279.9 0.0 collective-permute-start.6
  279.9 2.1 reshape.41
  282.0 3.2 %collective-permute-done.6 = f32[32,120]{1,0:T(8,128)S(1)} collective-permute-done((f32[32,120]{1,0:T(8,128)S(1)}, f32[32,120]{1,0:T(8,128)S(1)}, u32[]{:S(2)}, u32[]{:S(2)}) %collective-permute-start.6) | collective-permute-done | bytes 15392 | tf_op jit(solution)/shard_map/ppermute | solution.py:99
  285.2 0.6 add.84
  (16 shorter events, 0.1 us)
Async XLA Ops:
  7.2 9.6 %copy-start = (bf16[120,8,1440]{2,1,0:T(8,128)(2,1)S(1)}, bf16[120,8,1440]{2,1,0:T(8,128)(2,1)}, u32[]{:S(2)}) copy-start(bf16[120,8,1440]{2,1,0:T(8,128)(2,1)} %param.5) | copy-start | bytes 8294404
  7.2 120.6 %all-reduce.2.cloned.1.call-start = ((), (), s32[]{:S(2)}) async-start(), calls=%async_computation | async-start | bytes 2949120 | tf_op jit(solution)/shard_map/psum | solution.py:88
  12.0 12.4 %collective-permute-start = (bf16[120,1,1440]{2,0,1:T(8,128)(2,1)}, bf16[120,1,1440]{2,0,1:T(8,128)(2,1)}, u32[]{:S(2)}, u32[]{:S(2)}) collective-permute-start(bf16[120,1,1440]{2,0,1:T(8,128)(2,1)} %copy.21), channel_id=1, source_target_pairs={{0,1},{1,2},{2,3},{3,4},{4,5},{5,6},{6,7},{7,8},{8,9},{9,10},{10,1... | collective-permute-start | bytes 1036808 | tf_op jit(solution)/shard_map/ppermute | solution.py:17
  15.4 10.7 %collective-permute-start.1 = (bf16[120,1,1440]{2,0,1:T(8,128)(2,1)}, bf16[120,1,1440]{2,0,1:T(8,128)(2,1)}, u32[]{:S(2)}, u32[]{:S(2)}) collective-permute-start(bf16[120,1,1440]{2,0,1:T(8,128)(2,1)} %copy.22), channel_id=1, source_target_pairs={{1,0},{2,1},{3,2},{4,3},{5,4},{6,5},{7,6},{8,7},{9,8},{10,9},{11,1... | collective-permute-start | bytes 1036808 | tf_op jit(solution)/shard_map/ppermute | solution.py:19
  16.7 6.9 %copy-start.3 = (s32[120]{0:T(128)S(1)}, s32[120]{0:T(128)}, u32[]{:S(2)}) copy-start(s32[120]{0:T(128)} %param.7) | copy-start | bytes 1444
  22.7 5.1 %copy-start.1 = (bf16[120,8,1440]{2,1,0:T(8,128)(2,1)S(1)}, bf16[120,8,1440]{2,1,0:T(8,128)(2,1)}, u32[]{:S(2)}) copy-start(bf16[120,8,1440]{2,1,0:T(8,128)(2,1)} %param.4) | copy-start | bytes 8294404
  26.1 5.3 %slice-start = ((s8[5898240]{0:T(1024)(128)(4,1)}), s8[4194304]{0:T(1024)(128)(4,1)S(1)}, s32[]{:S(2)}) async-start(s8[5898240]{0:T(1024)(128)(4,1)} %bitcast.18), calls=%async_computation.1 | async-start | bytes 8388608
  27.8 3.5 %slice-start.1 = ((s8[5898240]{0:T(1024)(128)(4,1)}), s8[1703936]{0:T(1024)(128)(4,1)S(1)}, s32[]{:S(2)}) async-start(s8[5898240]{0:T(1024)(128)(4,1)} %bitcast.18), calls=%async_computation.2 | async-start | bytes 3407872
  27.8 3.5 %copy-start.2 = (f32[120,8,1]{2,1,0:T(8,128)S(1)}, f32[120,8,1]{2,1,0:T(8,128)}, u32[]{:S(2)}) copy-start(f32[120,8,1]{2,1,0:T(8,128)} %get-tuple-element.3) | copy-start | bytes 11524
  265.9 1.3 collective-permute-start.2
  267.2 3.7 %collective-permute-start.3 = (f32[32,120]{1,0:T(8,128)S(1)}, f32[32,120]{1,0:T(8,128)S(1)}, u32[]{:S(2)}, u32[]{:S(2)}) collective-permute-start(f32[32,120]{1,0:T(8,128)S(1)} %add.80), channel_id=1, source_target_pairs={{0,2},{1,3},{2,0},{3,1},{4,6},{5,7},{6,4},{7,5},{8,10},{9,11},{10,... | collective-permute-start | bytes 46088 | tf_op jit(solution)/shard_map/ppermute | solution.py:99
  270.9 5.2 %collective-permute-start.4 = (f32[32,120]{1,0:T(8,128)S(1)}, f32[32,120]{1,0:T(8,128)S(1)}, u32[]{:S(2)}, u32[]{:S(2)}) collective-permute-start(f32[32,120]{1,0:T(8,128)S(1)} %add.81), channel_id=1, source_target_pairs={{0,4},{1,5},{2,6},{3,7},{4,0},{5,1},{6,2},{7,3},{8,12},{9,13},{10,... | collective-permute-start | bytes 46088 | tf_op jit(solution)/shard_map/ppermute | solution.py:99
  276.2 3.7 %collective-permute-start.5 = (f32[32,120]{1,0:T(8,128)S(1)}, f32[32,120]{1,0:T(8,128)S(1)}, u32[]{:S(2)}, u32[]{:S(2)}) collective-permute-start(f32[32,120]{1,0:T(8,128)S(1)} %add.82), channel_id=1, source_target_pairs={{0,8},{1,9},{2,10},{3,11},{4,12},{5,13},{6,14},{7,15},{8,0},{9,1},... | collective-permute-start | bytes 46088 | tf_op jit(solution)/shard_map/ppermute | solution.py:99
  279.9 5.2 %collective-permute-start.6 = (f32[32,120]{1,0:T(8,128)S(1)}, f32[32,120]{1,0:T(8,128)S(1)}, u32[]{:S(2)}, u32[]{:S(2)}) collective-permute-start(f32[32,120]{1,0:T(8,128)S(1)} %add.83), channel_id=1, source_target_pairs={{0,16},{1,17},{2,18},{3,19},{4,20},{5,21},{6,22},{7,23},{8,24},{9,... | collective-permute-start | bytes 46088 | tf_op jit(solution)/shard_map/ppermute | solution.py:99
Sparse Core Ops, SparseCore 0:
  45.5 82.2 all-reduce.1
